TPU v7x, 256 devices: a whole 4x4x8 slice. The times are simulated.
256 devices in a mesh: section: 16 (over y_hi, x, core), expert: 16 (over z, y_lo).
Axes of the slice: x: 4, y: 4 (y_hi: 2, y_lo: 2; y = y_hi * 2 + y_lo), z: 8, core: 2. Of those that a mesh axis runs over, the one named last changes fastest.
Arguments:
- cotangent: bfloat16 [16, 2048, 4096], P('section', 'expert'), may hold values from -6 to 6
- routes: int32 [16, 2048, 2], P('section', 'expert'), may hold values from 0 to 15, all different within a row; in each aligned block of 64 rows (0 to 63, 64 to 127, ..., all dimensions but the last counted through in order) at most 16 rows name the same one
- gate_prob: float32 [16, 2048, 2], P('section', 'expert'), may hold values from 0.05 to 1
- hidden: bfloat16 [16, 16, 2, 16, 16, 1536], P('section', 'expert'), may hold values from -6 to 6
Outputs:
- grad_pair: bfloat16 [8, 16, 1536, 4096], P(None, 'expert', 'section')
Inputs may be any that keep to these rules, and one draw needn't show every extreme that they name: `routes`: each row names 2 different experts. In each aligned block of 64 rows (one micro-batch of one device) no expert is named by more than 16 rows.
All inputs are finite; a program needn't handle non-finite values.
Results may differ from a plain program's by a relative error of at most 0.0059.
Values may be sent and summed in bfloat16 or wider, within the bound.
A program may use at most 128 MiB of HBM per device.

v0:
```python
from functools import partial
import jax
import jax.numpy as jnp
from jax import lax
from jax.sharding import PartitionSpec as P


def slot_index(route_blk, experts_total):
    labels = jnp.arange(experts_total, dtype=jnp.int32)
    hits = (route_blk[:, :, None] == labels).astype(jnp.int32)
    per_token = jnp.sum(hits, axis=1)
    before = jnp.cumsum(per_token, axis=0) - per_token
    return jnp.sum(hits * before[:, None, :], axis=2)


def pack_block(cot_blk, route_blk, prob_blk, experts_total, capacity):
    width = cot_blk.shape[1]
    slots = slot_index(route_blk, experts_total)
    flat = (route_blk * capacity + slots).reshape(-1)
    weighted = (prob_blk[:, :, None] * cot_blk[:, None, :].astype(jnp.float32)).astype(jnp.bfloat16)
    empty = jnp.zeros((experts_total * capacity, width), jnp.bfloat16)
    return empty.at[flat].set(weighted.reshape(-1, width)).reshape(experts_total, capacity, width)


def rows_product(acts, arrived):
    return lax.dot_general(
        acts, arrived, (((0,), (0,)), ((), ())), preferred_element_type=jnp.float32
    )


def pair_add(pieces, half):
    lower = pieces[:half].astype(jnp.float32)
    upper = jnp.flip(pieces[half:], 0).astype(jnp.float32)
    return (lower + upper).astype(jnp.bfloat16)


def local(cotangent, routes, gate_prob, hidden):
    n_section = lax.axis_size("section")
    half = n_section // 2
    mb_count = hidden.shape[2]
    sources = hidden.shape[3]
    capacity = hidden.shape[4]
    ff_width = hidden.shape[5]
    width = cotangent.shape[2]
    top_count = routes.shape[2]
    tok_block = cotangent.shape[1] // mb_count
    cot_blocks = cotangent.reshape(mb_count, tok_block, width)
    route_blocks = routes.reshape(mb_count, tok_block, top_count)
    prob_blocks = gate_prob.reshape(mb_count, tok_block, top_count)
    packer = partial(pack_block, experts_total=sources, capacity=capacity)
    packed = jax.vmap(packer)(cot_blocks, route_blocks, prob_blocks)
    acts = hidden.reshape(mb_count * sources * capacity, ff_width)
    arrived = lax.all_to_all(packed, "expert", split_axis=1, concat_axis=1, tiled=True)
    rows = arrived.reshape(mb_count * sources * capacity, width)
    part = rows_product(acts, rows).astype(jnp.bfloat16)
    pieces = lax.all_to_all(part[None], "section", split_axis=1, concat_axis=0, tiled=True)
    result = pair_add(pieces, half)
    return result[:, None]


def solution(mesh):
    return jax.shard_map(
        local,
        mesh=mesh,
        in_specs=(
            P("section", "expert", None),
            P("section", "expert", None),
            P("section", "expert", None),
            P("section", "expert", None, None, None, None),
        ),
        out_specs=P(None, "expert", "section", None),
        check_vma=False,
    )
```

profile of v0, /device:TPU:1, one launch (start us, length us, event | category | flops | bytes accessed | tf_op | source)
XLA Modules:
  0.0 582.4 jit_solution(12022639161730682039)
XLA Ops:
  0.0 0.9 eq.15
  0.9 0.7 broadcast_multiply_fusion
  1.6 0.1 copy.30
  1.7 0.1 reduce_window_sum.11
  1.8 0.1 copy.32
  1.9 0.1 copy.33
  2.0 0.1 reduce_sum.22
  2.1 0.1 copy.28
  2.2 0.1 mul.45
  2.4 5.3 mul.50
  7.7 6.1 %mul.51 = f32[2,128,4096]{2,1,0:T(8,128)} reshape(f32[2,64,2,4096]{3,2,1,0:T(2,128)} %mul.50) | data formatting | bytes 8388608 | tf_op jit(solution)/shard_map/vmap()/mul | solution.py:20
  13.8 0.1 copy.34
  13.9 0.1 mul.48
  14.1 4.0 multiply_convert_fusion
  18.1 2.5 broadcast_in_dim.12
  20.6 66.4 %scatter_fusion = bf16[2,256,4096]{2,1,0:T(8,128)(2,1)} fusion(bf16[2,256,4096]{2,1,0:T(8,128)(2,1)} %broadcast_in_dim.12, s32[256]{0:T(256)S(1)} %fusion.5, bf16[256,4096]{1,0:T(8,128)(2,1)} %bitcast.36), kind=kCustom, calls=%fused_computation | custom fusion | bytes 6293504 | tf_op jit(solution)/shard_map/vmap()/scatter | solution.py:22
  87.0 2.5 copy.35
  89.5 104.1 %all_to_all.17 = bf16[2,16,16,4096]{3,2,0,1:T(8,128)(2,1)S(1)} all-to-all(bf16[2,16,16,4096]{3,2,0,1:T(8,128)(2,1)S(1)} %copy.35), channel_id=1, replica_groups=mesh['section'=16,'expert'=16] {'expert'}, dimensions={1} | all-to-all | bytes 8388608 | tf_op jit(solution)/shard_map/all_to_all | solution.py:53
  193.6 0.5 copy.36
  194.1 0.0 copy-done
  194.1 9.7 %fusion = bf16[1,1536,4096]{1,2,0:T(8,128)(2,1)} fusion(bf16[512,4096]{1,0:T(8,128)(2,1)S(1)} %bitcast.37, bf16[512,1536]{1,0:T(8,128)(2,1)S(1)} %bitcast.29), kind=kOutput, calls=%fused_computation.2 | convolution fusion | flops 6448742400 | bytes 18350080 | tf_op jit(solution)/shard_map/dot_general | solution.py:26
  203.8 54.3 %copy.37 = bf16[1,1536,4096]{2,0,1:T(2,128)(2,1)} copy(bf16[1,1536,4096]{1,2,0:T(8,128)(2,1)} %fusion) | data formatting | bytes 25165824 | tf_op jit(solution)/shard_map/broadcast_in_dim | solution.py:56
  258.1 0.5 broadcast.51
  258.6 77.6 %reduce = bf16[1536,4096]{1,0:T(8,128)(2,1)} reduce(bf16[1536,1,4096]{2,1,0:T(2,128)(2,1)} %bitcast.33, bf16[]{:T(256)} %broadcast.51), dimensions={1}, to_apply=%bitcast.25.reduce_sub_computation | reduce | bytes 25165826
  336.2 17.6 %reshape.86 = bf16[16,2,196608]{2,1,0:T(2,128)(2,1)} reshape(bf16[1536,4096]{1,0:T(8,128)(2,1)} %reduce) | data formatting | bytes 25165824
  353.8 149.8 %all_to_all.18 = bf16[16,2,196608]{2,1,0:T(2,128)(2,1)} all-to-all(bf16[16,2,196608]{2,1,0:T(2,128)(2,1)} %reshape.86), channel_id=1, replica_groups=mesh['section'=16,'expert'=16] {'section'}, dimensions={0} | all-to-all | bytes 25165824 | tf_op jit(solution)/shard_map/all_to_all | solution.py:56
  503.6 20.6 %reshape.87 = bf16[1536,1,4096]{2,1,0:T(2,128)(2,1)} reshape(bf16[16,2,196608]{2,1,0:T(2,128)(2,1)} %all_to_all.18) | data formatting | bytes 25165824
  524.2 15.5 %slice.16 = bf16[1,768,4096]{2,0,1:T(2,128)(2,1)} slice(bf16[1,1536,4096]{2,0,1:T(2,128)(2,1)} %bitcast.30), slice={[0:1], [768:1536], [0:4096]} | slice | bytes 12582912 | tf_op jit(solution)/shard_map/slice | solution.py:33
  539.7 0.7 copy-done.2
  540.4 17.1 %copy.40 = bf16[1,1536,4096]{2,1,0:T(8,128)(2,1)} copy(bf16[1,1536,4096]{2,0,1:T(2,128)(2,1)S(1)} %bitcast.31) | data formatting | bytes 25165824
  557.5 14.4 %copy.41 = bf16[1,768,4096]{2,1,0:T(8,128)(2,1)} copy(bf16[1,768,4096]{2,0,1:T(2,128)(2,1)} %slice.16) | data formatting | bytes 12582912
  571.9 10.5 %fusion.2 = bf16[8,1,96,4096]{3,2,1,0:T(8,128)(2,1)} fusion(bf16[1,16,96,4096]{3,2,1,0:T(8,128)(2,1)} %bitcast.34, bf16[8,96,4096]{2,1,0:T(8,128)(2,1)} %bitcast.35), kind=kLoop, calls=%fused_computation.5 | loop fusion | flops 12582912 | bytes 18874368 | tf_op jit(solution)/shard_map/broadcast_in_dim | solution.py:58
  (11 shorter events, 0.1 us)
Async XLA Ops:
  0.0 194.1 %copy-start = (bf16[1,1,2,16,16,1536]{5,4,3,2,1,0:T(8,128)(2,1)S(1)}, bf16[1,1,2,16,16,1536]{5,4,3,2,1,0:T(8,128)(2,1)}, u32[]{:S(2)}) copy-start(bf16[1,1,2,16,16,1536]{5,4,3,2,1,0:T(8,128)(2,1)} %param.7) | copy-start | bytes 4718596
  7.7 6.1 %copy-start.3 = (f32[1,128,2]{1,2,0:T(2,128)S(1)}, f32[1,128,2]{1,2,0:T(2,128)}, u32[]{:S(2)}) copy-start(f32[1,128,2]{1,2,0:T(2,128)} %param.6) | copy-start | bytes 3076
  524.2 16.2 %copy-start.2 = (bf16[1536,1,4096]{2,1,0:T(2,128)(2,1)S(1)}, bf16[1536,1,4096]{2,1,0:T(2,128)(2,1)}, u32[]{:S(2)}) copy-start(bf16[1536,1,4096]{2,1,0:T(2,128)(2,1)} %reshape.87) | copy-start | bytes 37748740
  571.9 10.6 %copy-start.1 = (bf16[1,1,2,16,16,1536]{5,4,3,2,1,0:T(8,128)(2,1)S(1)}, bf16[1,1,2,16,16,1536]{5,4,3,2,1,0:T(8,128)(2,1)}, u32[]{:S(2)}) copy-start(bf16[1,1,2,16,16,1536]{5,4,3,2,1,0:T(8,128)(2,1)} %param.7) | copy-start | bytes 4718596
where the time goes:
time: 586 us; the launch traced here: 582 us
  blocking collectives  254 us (43%)
  local copies, waits for them, and re-layouts  226 us (39%)
  other arithmetic  93 us (16%)
  matrix products  9.71 us (2%)
    all_to_all x1, blocking collectives, local(): lax.all_to_all(part[None], 'section', split_axis=1, concat_axis=0, tiled=...  150 us
    all_to_all x1, blocking collectives, local(): lax.all_to_all(packed, 'expert', split_axis=1, concat_axis=1, tiled=True)  104 us
    unnamed x1, other arithmetic  77.6 us
    unnamed x14, local copies, waits for them, and re-layouts  71 us
    scatter x1, local copies, waits for them, and re-layouts, pack_block(): empty.at[flat].set(weighted.reshape(-1, width))  66.4 us
    broadcast_in_dim x1, local copies, waits for them, and re-layouts, local(): part[None]  54.3 us
    slice x1, local copies, waits for them, and re-layouts, pair_add(): upper = jnp.flip(pieces[half:], 0).astype(jnp.float32)  15.5 us

commit v1 on v0

--- a/solution.py
+++ b/solution.py
@@ -53,7 +53,12 @@
     arrived = lax.all_to_all(packed, "expert", split_axis=1, concat_axis=1, tiled=True)
     rows = arrived.reshape(mb_count * sources * capacity, width)
     part = rows_product(acts, rows).astype(jnp.bfloat16)
-    pieces = lax.all_to_all(part[None], "section", split_axis=1, concat_axis=0, tiled=True)
+    pieces = jnp.concatenate(
+        lax.all_to_all(
+            jnp.stack(jnp.split(part[None], lax.axis_size("section"), axis=1)), "section", 0, 0
+        ),
+        axis=0,
+    )
     result = pair_add(pieces, half)
     return result[:, None]
 

time: 586 us -> 371 us (0.63)
  local copies, waits for them, and re-layouts: 226 us -> 93.9 us
  other arithmetic: 93 us -> 15.4 us
    unnamed x1 -> x0, other arithmetic: 77.6 us -> none
    unnamed x14 -> x22, local copies, waits for them, and re-layouts: 71 us -> 6.16 us
    broadcast_in_dim x1 -> x0, local copies, waits for them, and re-layouts: 54.3 us -> none  [local(): part[None]]
    slice x1, local copies, waits for them, and re-layouts: 15.5 us -> 3.03 us  [pair_add(): upper = jnp.flip(pieces[half:], 0).astype(jnp.float32)]
where the time goes in v1:
time: 371 us; the launch traced here: 370 us
  blocking collectives  254 us (68%)
  local copies, waits for them, and re-layouts  93.9 us (25%)
  other arithmetic  15.4 us (4%)
  matrix products  7.26 us (2%)
    all_to_all x1, blocking collectives, local(): lax.all_to_all(jnp.stack(jnp.split(part[None], lax.axis_size('section'),...  149 us
    all_to_all x1, blocking collectives, local(): lax.all_to_all(packed, 'expert', split_axis=1, concat_axis=1, tiled=True)  104 us
    scatter x1, local copies, waits for them, and re-layouts, pack_block(): empty.at[flat].set(weighted.reshape(-1, width))  66.4 us
    mul x3, local copies, waits for them, and re-layouts, pack_block(): prob_blk[:, :, None] * cot_blk[:, None, :].astype(jnp.float32)  11.5 us
    broadcast_in_dim x1, other arithmetic, local(): return result[:, None]  10.4 us

profile of v1, /device:TPU:1, one launch (start us, length us, event | category | flops | bytes accessed | tf_op | source)
XLA Modules:
  0.0 370.3 jit_solution(7911290514789984910)
XLA Ops:
  0.0 0.8 broadcast_multiply_fusion
  0.8 0.8 eq.15
  1.6 0.1 copy.27
  1.7 0.1 copy.25
  1.8 0.1 mul.45
  1.9 0.1 reduce_window_sum.11
  2.0 0.1 copy.29
  2.1 0.1 copy.30
  2.2 0.1 reduce_sum.22
  2.4 0.8 copy.31
  3.2 0.1 mul.48
  3.3 5.3 %mul.50 = f32[2,64,2,4096]{3,2,1,0:T(2,128)} broadcast(bf16[2,64,4096]{2,1,0:T(8,128)(2,1)} %bitcast.98), dimensions={0,1,3} | broadcast | bytes 5242880 | tf_op jit(solution)/shard_map/vmap()/mul | solution.py:20
  8.7 6.1 %mul.51 = f32[2,128,4096]{2,1,0:T(8,128)} reshape(f32[2,64,2,4096]{3,2,1,0:T(2,128)} %mul.50) | data formatting | bytes 8388608 | tf_op jit(solution)/shard_map/vmap()/mul | solution.py:20
  14.7 4.0 %multiply_convert_fusion = bf16[2,128,4096]{2,1,0:T(8,128)(2,1)} fusion(f32[2,128,4096]{2,1,0:T(8,128)} %mul.51, f32[2,128]{1,0:T(2,128)S(1)} %mul.48), kind=kLoop, calls=%fused_computation.8 | loop fusion | flops 2097152 | bytes 6292480 | tf_op jit(solution)/shard_map/vmap()/convert_element_type | solution.py:20
  18.7 2.5 broadcast_in_dim.12
  21.2 66.4 %scatter_fusion = bf16[2,256,4096]{2,1,0:T(8,128)(2,1)} fusion(bf16[2,256,4096]{2,1,0:T(8,128)(2,1)} %broadcast_in_dim.12, s32[256]{0:T(256)S(1)} %fusion.21, bf16[256,4096]{1,0:T(8,128)(2,1)} %bitcast.96), kind=kCustom, calls=%fused_computation | custom fusion | bytes 6293504 | tf_op jit(solution)/shard_map/vmap()/scatter | solution.py:22
  87.7 2.5 copy.32
  90.1 104.3 %all_to_all.10 = bf16[2,16,16,4096]{3,2,0,1:T(8,128)(2,1)S(1)} all-to-all(bf16[2,16,16,4096]{3,2,0,1:T(8,128)(2,1)S(1)} %copy.32), channel_id=1, replica_groups=mesh['section'=16,'expert'=16] {'expert'}, dimensions={1} | all-to-all | bytes 8388608 | tf_op jit(solution)/shard_map/all_to_all | solution.py:53
  194.4 0.3 copy.33
  194.7 7.3 %fusion = bf16[1,1536,4096]{2,1,0:T(8,128)(2,1)S(1)} fusion(bf16[512,4096]{1,0:T(8,128)(2,1)S(1)} %bitcast.97, bf16[512,1536]{1,0:T(8,128)(2,1)S(1)} %bitcast.93), kind=kOutput, calls=%fused_computation.2 | convolution fusion | flops 6448742400 | bytes 18350080 | tf_op jit(solution)/shard_map/dot_general | solution.py:26
  202.0 0.1 fusion.17
  202.1 0.1 fusion.16
  202.1 0.1 fusion.15
  202.2 0.1 fusion.14
  202.3 0.1 fusion.13
  202.4 0.1 fusion.11
  202.4 0.1 fusion.10
  202.5 0.1 fusion.9
  202.9 149.4 %all_to_all.11 = bf16[16,1,96,4096]{3,2,1,0:T(8,128)(2,1)S(1)} all-to-all(bf16[16,1,96,4096]{3,2,1,0:T(8,128)(2,1)S(1)} %fusion.3), channel_id=1, replica_groups=mesh['section'=16,'expert'=16] {'section'}, dimensions={0} | all-to-all | bytes 25165824 | tf_op jit(solution)/shard_map/all_to_all | solution.py:57
  352.3 4.6 %copy-done.2 = bf16[16,1,96,4096]{3,2,1,0:T(8,128)(2,1)} copy-done((bf16[16,1,96,4096]{3,2,1,0:T(8,128)(2,1)}, bf16[16,1,96,4096]{3,2,1,0:T(8,128)(2,1)S(1)}, u32[]{:S(2)}) %copy-start.2) | copy-done | bytes 12582936
  356.9 3.0 slice_bitcast_fusion
  359.9 10.4 %fusion.2 = bf16[8,1,96,4096]{3,2,1,0:T(8,128)(2,1)} fusion(bf16[16,1,96,4096]{3,2,0,1:T(8,128)(2,1)} %bitcast.95, bf16[8,96,4096]{2,1,0:T(8,128)(2,1)} %slice_bitcast_fusion), kind=kLoop, calls=%fused_computation.5 | loop fusion | flops 12582912 | bytes 18874368 | tf_op jit(solution)/shard_map/broadcast_in_dim | solution.py:63
  (18 shorter events, 0.5 us)
Async XLA Ops:
  0.0 194.7 %copy-start = (bf16[1,1,2,16,16,1536]{5,4,3,2,1,0:T(8,128)(2,1)S(1)}, bf16[1,1,2,16,16,1536]{5,4,3,2,1,0:T(8,128)(2,1)}, u32[]{:S(2)}) copy-start(bf16[1,1,2,16,16,1536]{5,4,3,2,1,0:T(8,128)(2,1)} %param.7) | copy-start | bytes 4718596
  352.3 4.6 %copy-start.2 = (bf16[16,1,96,4096]{3,2,1,0:T(8,128)(2,1)}, bf16[16,1,96,4096]{3,2,1,0:T(8,128)(2,1)S(1)}, u32[]{:S(2)}) copy-start(bf16[16,1,96,4096]{3,2,1,0:T(8,128)(2,1)S(1)} %all_to_all.11) | copy-start | bytes 37748740
  356.9 13.5 %copy-start.1 = (bf16[1,1,2,16,16,1536]{5,4,3,2,1,0:T(8,128)(2,1)S(1)}, bf16[1,1,2,16,16,1536]{5,4,3,2,1,0:T(8,128)(2,1)}, u32[]{:S(2)}) copy-start(bf16[1,1,2,16,16,1536]{5,4,3,2,1,0:T(8,128)(2,1)} %param.7) | copy-start | bytes 4718596
